TPU v7x, 128 devices: a whole 4x4x4 slice. The times are simulated.
128 devices in a mesh: seq: 16 (over x, z), hx: 8 (over y, core).
Axes of the slice: x: 4, y: 4, z: 4, core: 2. Of those that a mesh axis runs over, the one named last changes fastest.
Arguments:
- query: bfloat16 [16384, 8192], P('seq', 'hx'), may hold values from -6 to 6
- key_in: bfloat16 [16384, 8192], P('seq', 'hx'), may hold values from -6 to 6
- value: bfloat16 [16384, 8192], P('seq', 'hx'), may hold values from -6 to 6
- head_gain: float32 [8192], P('hx'), may hold values from 0.1 to 1.9
- out_weight: bfloat16 [8192, 6144], P('hx', 'seq'), may hold values from -0.0625 to 0.0625
- residual: bfloat16 [16384, 6144], P(('seq', 'hx')), may hold values from -6 to 6
Outputs:
- mixed: bfloat16 [16384, 6144], P(('seq', 'hx'))
All inputs are finite; a program needn't handle non-finite values.
Results may differ from a plain program's by a relative error of at most 0.014.
Values may be sent and summed in bfloat16 or wider, within the bound.
No kernel may reach another device: no remote copies, remote signals or barrier semaphores. Data moves between devices by JAX's collectives and lax.ppermute only.
A program may use at most 128 MiB of HBM per device.

v0:
```python
import jax
import jax.numpy as jnp
from jax import lax
from jax.sharding import PartitionSpec as P

DH = 128


def activate(array):
    return jax.nn.silu(array.astype(jnp.float32)).astype(jnp.bfloat16)


def per_device(query, key_in, value, head_gain, out_weight, residual):
    highest = lax.Precision.HIGHEST
    tokens_here, width = query.shape
    heads = width // DH
    q_act = activate(query).reshape(tokens_here, heads, DH)
    k_act = activate(key_in).reshape(tokens_here, heads, DH)
    v_heads = value.reshape(tokens_here, heads, DH)
    blocks = min(512, tokens_here)
    count = tokens_here // blocks
    rows = jnp.arange(blocks, dtype=jnp.int32)
    lower = rows[:, None] >= rows[None, :]
    running = jnp.zeros((heads, DH, DH), jnp.float32)
    pieces = []
    for index in range(count):
        q_part = q_act[index * blocks : (index + 1) * blocks]
        k_part = k_act[index * blocks : (index + 1) * blocks]
        v_part = v_heads[index * blocks : (index + 1) * blocks]
        scores = jnp.einsum("thd,shd->hts", q_part, k_part, preferred_element_type=jnp.float32)
        scores = jnp.where(lower[None, :, :], scores, jnp.zeros_like(scores))
        inner = jnp.einsum("hts,she->the", scores, v_part.astype(jnp.float32), precision=highest)
        if index > 0:
            inner = inner + jnp.einsum(
                "thd,hde->the", q_part.astype(jnp.float32), running, precision=highest
            )
        pieces.append(inner)
        running = running + jnp.einsum(
            "thd,the->hde", k_part, v_part, preferred_element_type=jnp.float32
        )
    local_part = jnp.concatenate(pieces, axis=0)
    empty = jnp.zeros((heads, DH, DH), jnp.float32)
    position = lax.axis_index("seq")
    piece = lax.all_gather(running[None].astype(jnp.bfloat16), "seq", axis=0, tiled=True).astype(
        jnp.float32
    )
    ranks = jnp.arange(piece.shape[0], dtype=jnp.int32)
    keep = (ranks < position)[:, None, None, None]
    prefix = empty + jnp.sum(jnp.where(keep, piece, jnp.zeros_like(piece)), axis=0)
    attended = local_part + jnp.einsum(
        "thd,hde->the", q_act.astype(jnp.float32), prefix, precision=highest
    )
    meansq = jnp.mean(attended * attended, axis=-1, keepdims=True)
    normed = attended * lax.rsqrt(meansq + 1e-06) * head_gain.reshape(heads, DH)
    normed = normed.astype(jnp.bfloat16).reshape(tokens_here, width)
    full_weight = lax.all_gather(out_weight, "seq", axis=1, tiled=True)
    summed = lax.psum_scatter(
        jnp.dot(normed, full_weight, preferred_element_type=jnp.float32).astype(jnp.bfloat16),
        "hx",
        scatter_dimension=0,
        tiled=True,
    ).astype(jnp.float32)
    return (summed + residual.astype(jnp.float32)).astype(jnp.bfloat16)


def solution(mesh):
    return jax.shard_map(
        per_device,
        mesh=mesh,
        in_specs=(
            P("seq", "hx"),
            P("seq", "hx"),
            P("seq", "hx"),
            P("hx"),
            P("hx", "seq"),
            P(("seq", "hx"), None),
        ),
        out_specs=P(("seq", "hx"), None),
        check_vma=False,
    )
```

profile of v0, /device:TPU:1, one launch (start us, length us, event | category | flops | bytes accessed | tf_op | source)
XLA Modules:
  0.0 277.5 jit_solution(6667149055458355304)
XLA Ops:
  6.5 0.0 all-gather.6.cloned.1.call-start
  6.5 2.9 %copy.46 = bf16[1024,1024]{0,1:T(8,128)(2,1)S(1)} copy(bf16[1024,1024]{1,0:T(8,128)(2,1)} %param.7) | data formatting | bytes 4194304 | tf_op args[1]
  9.4 0.0 copy-start.9
  9.4 1.2 fusion.12
  10.6 1.1 fusion.25
  11.8 0.0 copy-done.9
  11.8 1.3 fusion.24
  13.1 0.5 copy.79
  13.6 0.0 copy-start.2
  13.6 1.9 copy.78
  15.5 0.0 copy-done
  15.5 0.4 fusion.28
  16.0 0.0 copy-start.7
  16.0 0.8 copy-done.7
  16.8 2.4 fusion.20
  19.2 0.0 all-gather.6.cloned.1.call-update
  19.2 0.0 all-gather.4.cloned.1.call-start
  19.2 0.7 all-gather.4.cloned.1.call-update
  19.9 0.0 copy-done.2
  19.9 0.0 reduce-scatter.2.cloned.1.call-start
  20.0 4.0 %copy.45 = bf16[1024,1024]{0,1:T(8,128)(2,1)} copy(bf16[1024,1024]{1,0:T(8,128)(2,1)} %param.6) | data formatting | bytes 4194304 | tf_op args[0]
  24.0 0.1 iota_compare_fusion
  24.0 0.0 copy-start.4
  24.1 2.9 %fusion.8 = bf16[1024,1024]{0,1:T(8,128)(2,1)S(1)} fusion(bf16[1024,1024]{0,1:T(8,128)(2,1)} %copy.45), kind=kLoop, calls=%fused_computation.14 | loop fusion | flops 6291456 | bytes 4194304 | tf_op jit(solution)/shard_map/convert_element_type | solution.py:10
  27.0 0.1 fusion.23
  27.1 0.0 copy-done.4
  27.1 0.0 copy-start.3
  27.1 1.3 fusion.27
  28.4 0.0 copy-done.3
  28.4 0.0 copy-start.8
  28.4 4.5 %fusion.1 = f32[8,512,128]{2,1,0:T(8,128)S(1)} fusion(bf16[512,8,128]{0,2,1:T(8,128)(2,1)S(1)} %bitcast.41, f32[8,512,512]{2,1,0:T(8,128)S(1)} %fusion.27, pred[512,512]{1,0:T(8,128)(4,1)S(1)} %iota_compare_fusion), kind=kOutput, calls=%fused_computation.3 | convolution fusion | flops 3223322624 | bytes 11796480 | tf_op jit(solution)/shard_map/hts,she->the/dot_general | solution.py:32
  33.0 0.0 copy-done.8
  33.0 0.0 copy-start.1
  33.0 2.5 bitcast_add_fusion
  35.5 0.0 copy-done.1
  35.5 1.3 fusion.26
  36.8 6.0 %fusion.17 = f32[512,8,128]{2,0,1:T(8,128)} fusion(bf16[512,8,128]{0,2,1:T(8,128)(2,1)S(1)} %bitcast.37, f32[8,512,512]{2,1,0:T(8,128)S(1)} %fusion.26, pred[512,512]{1,0:T(8,128)(4,1)S(1)} %iota_compare_fusion), kind=kOutput, calls=%fused_computation.28 | convolution fusion | flops 3223322624 | bytes 11796480 | tf_op jit(solution)/shard_map/hts,she->the/dot_general | solution.py:32
  42.8 31.4 %all-gather.6.cloned.1.call-done = bf16[128,128,128]{2,1,0:T(8,128)(2,1)} async-done(((bf16[8,128,128]{2,1,0:T(8,128)(2,1)}), bf16[128,128,128]{2,1,0:T(8,128)(2,1)}) %all-gather.6.cloned.1.call-update) | async-done | bytes 4194320 | tf_op jit(solution)/shard_map/all_gather | solution.py:44
  74.2 3.3 %fusion = f32[8,128,128]{2,1,0:T(8,128)S(1)} fusion(bf16[16,8,128,128]{3,2,1,0:T(8,128)(2,1)} %bitcast.46, pred[16]{0:T(512)(128)(4,1)S(1)} %iota_compare_fusion.1), kind=kLoop, calls=%fused_computation.2 | loop fusion | flops 6160384 | bytes 4718608 | tf_op jit(solution)/shard_map/reduce_sum | solution.py:49
  77.6 0.1 copy-done.6
  77.7 3.3 %multiply_reduce_fusion = (f32[1024,8]{0,1:T(8,128)S(1)}, f32[1024,8,128]{2,0,1:T(8,128)S(1)}) fusion(f32[8,128,128]{2,1,0:T(8,128)S(1)} %fusion, bf16[1024,8,128]{0,2,1:T(8,128)(2,1)S(1)} %bitcast.35, f32[512,8,128]{2,0,1:T(8,128)S(1)} %copy-done.5, f32[512,8,128]{2,0,1:T(8,128)S(1)} %copy-done.6), kind=kOutput, calls=%fused_computation.21 | convolution fusion | flops 1614798848 | bytes 11042816 | tf_op jit(solution)/shard_map/thd,hde->the/dot_general | solution.py:50
  81.0 1.4 multiply_convert_fusion
  82.4 2.7 copy.63
  85.2 89.7 %all-gather.4.cloned.1.call-done = bf16[1024,6144]{1,0:T(8,128)(2,1)} async-done(((bf16[1024,384]{1,0:T(8,128)(2,1)}), bf16[1024,6144]{1,0:T(8,128)(2,1)}) %all-gather.4.cloned.1.call-update) | async-done | bytes 12582928 | tf_op jit(solution)/shard_map/all_gather | solution.py:56
  174.9 21.1 %convolution_convert_fusion = bf16[1024,6144]{1,0:T(8,128)(2,1)} fusion(bf16[1024,1024]{0,1:T(8,128)(2,1)} %bitcast.48, bf16[1024,6144]{1,0:T(8,128)(2,1)} %all-gather.4.cloned.1.call-done), kind=kOutput, calls=%fused_computation | convolution fusion | flops 12891193344 | bytes 27262976 | tf_op jit(solution)/shard_map/dot_general | solution.py:58
  195.9 0.0 reduce-scatter.2.cloned.1.call-update
  195.9 72.1 %reduce-scatter.2.cloned.1.call-done = bf16[128,6144]{1,0:T(8,128)(2,1)} async-done(((bf16[1024,6144]{1,0:T(8,128)(2,1)}), bf16[128,6144]{1,0:T(8,128)(2,1)}) %reduce-scatter.2.cloned.1.call-update) | async-done | bytes 1572880 | tf_op jit(solution)/shard_map/reduce_scatter | solution.py:57
  268.0 2.9 %add_convert_fusion = bf16[128,6144]{1,0:T(8,128)(2,1)} fusion(bf16[128,6144]{1,0:T(8,128)(2,1)S(1)} %copy-done.10, bf16[128,6144]{1,0:T(8,128)(2,1)} %reduce-scatter.2.cloned.1.call-done), kind=kLoop, calls=%fused_computation.26 | loop fusion | flops 3145728 | bytes 4718592 | tf_op jit(solution)/shard_map/convert_element_type | solution.py:63
  (10 shorter events, 0.0 us)
Async XLA Ops:
  6.5 67.7 %all-gather.6.cloned.1.call-start = ((), (), s32[]{:S(2)}) async-start(), calls=%async_computation.3 | async-start | bytes 4456448 | tf_op jit(solution)/shard_map/all_gather | solution.py:44
  9.4 2.4 copy-start.9
  11.8 3.8 %copy-start = (bf16[512,1024]{0,1:T(8,128)(2,1)}, bf16[512,1024]{0,1:T(8,128)(2,1)S(1)}, u32[]{:S(2)}) copy-start(bf16[512,1024]{0,1:T(8,128)(2,1)S(1)} %get-tuple-element.9) | copy-start | bytes 3145732
  13.6 6.3 %copy-start.2 = (bf16[512,1024]{0,1:T(8,128)(2,1)}, bf16[512,1024]{0,1:T(8,128)(2,1)S(1)}, u32[]{:S(2)}) copy-start(bf16[512,1024]{0,1:T(8,128)(2,1)S(1)} %copy.79) | copy-start | bytes 3145732
  16.0 0.8 copy-start.7
  19.2 155.7 %all-gather.4.cloned.1.call-start = ((), (), s32[]{:S(2)}) async-start(), calls=%async_computation.1 | async-start | bytes 13369344 | tf_op jit(solution)/shard_map/all_gather | solution.py:56
  19.9 248.1 %reduce-scatter.2.cloned.1.call-start = ((), (), s32[]{:S(2)}) async-start(), calls=%async_computation.2 | async-start | bytes 14155776 | tf_op jit(solution)/shard_map/reduce_scatter | solution.py:57
  24.0 3.1 %copy-start.4 = (bf16[512,1024]{0,1:T(8,128)(2,1)S(1)}, bf16[512,1024]{0,1:T(8,128)(2,1)}, u32[]{:S(2)}) copy-start(bf16[512,1024]{0,1:T(8,128)(2,1)} %get-tuple-element.10) | copy-start | bytes 3145732
  27.1 1.3 copy-start.3
  28.4 4.6 %copy-start.8 = (f32[8,128,128]{2,1,0:T(8,128)S(1)}, f32[8,128,128]{2,1,0:T(8,128)}, u32[]{:S(2)}) copy-start(f32[8,128,128]{2,1,0:T(8,128)} %copy-done.7) | copy-start | bytes 1572868
  33.0 2.5 copy-start.1
  74.2 3.4 %copy-start.5 = (f32[512,8,128]{2,0,1:T(8,128)S(1)}, f32[512,8,128]{2,0,1:T(8,128)}, u32[]{:S(2)}) copy-start(f32[512,8,128]{2,0,1:T(8,128)} %bitcast_add_fusion) | copy-start | bytes 6291460
  74.2 3.5 %copy-start.6 = (f32[512,8,128]{2,0,1:T(8,128)S(1)}, f32[512,8,128]{2,0,1:T(8,128)}, u32[]{:S(2)}) copy-start(f32[512,8,128]{2,0,1:T(8,128)} %fusion.17) | copy-start | bytes 6291460
  77.7 3.3 %copy-start.11 = (f32[1024]{0:T(1024)S(1)}, f32[1024]{0:T(1024)}, u32[]{:S(2)}) copy-start(f32[1024]{0:T(1024)} %param.9) | copy-start | bytes 12292
  195.9 72.1 %copy-start.10 = (bf16[128,6144]{1,0:T(8,128)(2,1)S(1)}, bf16[128,6144]{1,0:T(8,128)(2,1)}, u32[]{:S(2)}) copy-start(bf16[128,6144]{1,0:T(8,128)(2,1)} %param.11) | copy-start | bytes 4718596
Sparse Core Ops, SparseCore 0:
  19.3 54.8 all-gather.5
  76.3 98.4 all-gather.3
  196.1 71.9 reduce-scatter.1
where the time goes:
time: 278 us; the launch traced here: 277 us
  waiting for transfers between devices  194 us (70%)
  matrix products  42.7 us (15%)
  local copies, waits for them, and re-layouts  15.5 us (6%)
  between operations  13.3 us (5%)
  other arithmetic  11.9 us (4%)
    all_gather x1, waiting for transfers between devices, per_device(): full_weight = lax.all_gather(out_weight, 'seq', axis=1, tiled=True)  89.7 us
    reduce_scatter x1, waiting for transfers between devices, per_device(): lax.psum_scatter(jnp.dot(normed, full_weight, preferred_element_type=jnp....  72.1 us
    all_gather x1, waiting for transfers between devices, per_device(): lax.all_gather(running[None].astype(jnp.bfloat16), 'seq', axis=0, tiled=T...  31.4 us
    dot_general x1, matrix products, per_device(): jnp.dot(normed, full_weight, preferred_element_type=jnp.float32)  21.1 us
    dot_general x2, matrix products, per_device(): jnp.einsum('hts,she->the', scores, v_part.astype(jnp.float32), precision=...  10.5 us
    unnamed x28, local copies, waits for them, and re-layouts  10.2 us
  transfers between devices with their start and end apart: 3, of which 3 were waited for; matrix products, arithmetic and copies ran while one was open for 12% of the time, Pallas kernels for 0%

commit v1 on v0

--- a/solution.py
+++ b/solution.py
@@ -4,6 +4,13 @@
 from jax.sharding import PartitionSpec as P
 
 DH = 128
+
+
+def exchange_gather(x, axis, dim):
+    size = lax.axis_size(axis)
+    blocks = jnp.stack([x for _ in range(size)])
+    blocks = lax.all_to_all(blocks, axis, split_axis=0, concat_axis=0)
+    return jnp.concatenate(blocks, axis=dim)
 
 
 def activate(array):
@@ -41,9 +48,7 @@
     local_part = jnp.concatenate(pieces, axis=0)
     empty = jnp.zeros((heads, DH, DH), jnp.float32)
     position = lax.axis_index("seq")
-    piece = lax.all_gather(running[None].astype(jnp.bfloat16), "seq", axis=0, tiled=True).astype(
-        jnp.float32
-    )
+    piece = exchange_gather(running[None].astype(jnp.bfloat16), "seq", 0).astype(jnp.float32)
     ranks = jnp.arange(piece.shape[0], dtype=jnp.int32)
     keep = (ranks < position)[:, None, None, None]
     prefix = empty + jnp.sum(jnp.where(keep, piece, jnp.zeros_like(piece)), axis=0)

time: 278 us -> 259 us (0.932)
  waiting for transfers between devices: 194 us -> 164 us
  starting transfers between devices: 0.08 us -> 8.52 us
    all_to_all x0 -> x1, waiting for transfers between devices: none -> 53.4 us  [exchange_gather(): blocks = lax.all_to_all(blocks, axis, split_axis=0, concat_axis=0)]
    all_gather x1, waiting for transfers between devices: 89.7 us -> 40.3 us  [per_device(): full_weight = lax.all_gather(out_weight, 'seq', axis=1, tiled=True)]
    all_gather x1 -> x0, waiting for transfers between devices: 31.4 us -> none  [per_device(): lax.all_gather(running[None].astype(jnp.bfloat16), 'seq', axis=0, tiled=T...]
    all_to_all x0 -> x1, starting transfers between devices: none -> 8.48 us  [exchange_gather(): blocks = lax.all_to_all(blocks, axis, split_axis=0, concat_axis=0)]
    another operation x0 -> x1, local copies, waits for them, and re-layouts: none -> 2.99 us  [exchange_gather(): blocks = jnp.stack([x for _ in range(size)])]
  transfers between devices with their start and end apart: 3 -> 3, of which waited for: 3 -> 3; matrix products, arithmetic and copies ran while one was open for 12% -> 18% of each run, Pallas kernels for 0% -> 0%
where the time goes in v1:
time: 259 us
  waiting for transfers between devices  164 us (63%)
  matrix products  40.8 us (16%)
  local copies, waits for them, and re-layouts  17.9 us (7%)
  between operations  13.6 us (5%)
  other arithmetic  13.5 us (5%)
  starting transfers between devices  8.52 us (3%)
    reduce_scatter x1, waiting for transfers between devices, per_device(): lax.psum_scatter(jnp.dot(normed, full_weight, preferred_element_type=jnp....  69.9 us
    all_to_all x1, waiting for transfers between devices, exchange_gather(): blocks = lax.all_to_all(blocks, axis, split_axis=0, concat_axis=0)  53.4 us
    all_gather x1, waiting for transfers between devices, per_device(): full_weight = lax.all_gather(out_weight, 'seq', axis=1, tiled=True)  40.3 us
    dot_general x1, matrix products, per_device(): jnp.dot(normed, full_weight, preferred_element_type=jnp.float32)  21 us
    dot_general x2, matrix products, per_device(): jnp.einsum('hts,she->the', scores, v_part.astype(jnp.float32), precision=...  10.5 us
    unnamed x28, local copies, waits for them, and re-layouts  10.2 us
    all_to_all x1, starting transfers between devices, exchange_gather(): blocks = lax.all_to_all(blocks, axis, split_axis=0, concat_axis=0)  8.48 us
    convert_element_type x2, other arithmetic, activate(): return jax.nn.silu(array.astype(jnp.float32)).astype(jnp.bfloat16)  5.7 us
  transfers between devices with their start and end apart: 3, of which 3 were waited for; matrix products, arithmetic and copies ran while one was open for 18% of the time, Pallas kernels for 0%

profile of v1, /device:TPU:1, one launch (start us, length us, event | category | flops | bytes accessed | tf_op | source)
XLA Modules:
  0.0 258.6 jit_solution(5963437819456066050)
XLA Ops:
  6.5 0.0 all-gather.2.cloned.1.call-start
  6.5 0.7 all-gather.2.cloned.1.call-update
  7.3 3.9 %copy.63 = bf16[1024,1024]{0,1:T(8,128)(2,1)} copy(bf16[1024,1024]{1,0:T(8,128)(2,1)} %param.7) | data formatting | bytes 4194304 | tf_op args[1]
  11.2 1.7 fusion.24
  12.9 0.5 copy.96
  13.5 0.0 copy-start
  13.5 0.5 copy.95
  14.0 2.8 %fusion.12 = bf16[1024,1024]{0,1:T(8,128)(2,1)S(1)} fusion(bf16[1024,1024]{0,1:T(8,128)(2,1)} %copy.63), kind=kLoop, calls=%fused_computation.18 | loop fusion | flops 6291456 | bytes 4194304 | tf_op jit(solution)/shard_map/convert_element_type | solution.py:17
  16.8 0.2 fusion.25
  17.0 0.0 copy-start.4
  17.0 0.0 copy-start.2
  17.0 0.4 fusion.28
  17.5 0.0 copy-start.8
  17.5 0.0 copy-done
  17.5 0.5 copy-done.4
  18.0 0.5 copy-done.8
  18.6 0.4 fusion.20
  19.0 3.0 %stack.2 = bf16[16,1,8,128,128]{4,3,2,1,0:T(8,128)(2,1)} broadcast(bf16[8,128,128]{2,1,0:T(8,128)(2,1)S(1)} %fusion.20), dimensions={2,3,4} | broadcast | bytes 4456448 | tf_op jit(solution)/shard_map/stack | solution.py:11
  22.0 0.0 copy-done.2
  22.0 8.5 %all-to-all-start = ((bf16[16,1,8,128,128]{4,3,2,1,0:T(8,128)(2,1)}), bf16[16,1,8,128,128]{4,3,2,1,0:T(8,128)(2,1)}, u32[]{:S(2)}, u32[]{:S(2)}) async-start(bf16[16,1,8,128,128]{4,3,2,1,0:T(8,128)(2,1)} %stack.2), calls=%async_computation | async-start | bytes 8388608 | tf_op jit(solution)/shard_map/all_to_all | solution.py:12
  30.5 0.0 reduce-scatter.2.cloned.1.call-start
  30.5 4.0 %copy.62 = bf16[1024,1024]{0,1:T(8,128)(2,1)} copy(bf16[1024,1024]{1,0:T(8,128)(2,1)} %param.6) | data formatting | bytes 4194304 | tf_op args[0]
  34.5 0.1 iota_compare_fusion
  34.6 0.0 copy-start.5
  34.6 2.9 %fusion.8 = bf16[1024,1024]{0,1:T(8,128)(2,1)S(1)} fusion(bf16[1024,1024]{0,1:T(8,128)(2,1)} %copy.62), kind=kLoop, calls=%fused_computation.14 | loop fusion | flops 6291456 | bytes 4194304 | tf_op jit(solution)/shard_map/convert_element_type | solution.py:17
  37.5 0.1 fusion.23
  37.7 0.0 copy-start.1
  37.7 1.3 fusion.27
  39.0 0.0 copy-done.1
  39.0 0.0 copy-start.9
  39.0 4.5 %fusion.1 = f32[8,512,128]{2,1,0:T(8,128)S(1)} fusion(bf16[512,8,128]{0,2,1:T(8,128)(2,1)S(1)} %bitcast.40, f32[8,512,512]{2,1,0:T(8,128)S(1)} %fusion.27, pred[512,512]{1,0:T(8,128)(4,1)S(1)} %iota_compare_fusion), kind=kOutput, calls=%fused_computation.3 | convolution fusion | flops 3223322624 | bytes 11796480 | tf_op jit(solution)/shard_map/hts,she->the/dot_general | solution.py:39
  43.5 0.0 copy-done.9
  43.6 0.0 copy-start.3
  43.6 2.5 bitcast_add_fusion
  46.1 0.0 copy-done.3
  46.1 1.3 fusion.26
  47.4 6.0 %fusion.17 = f32[512,8,128]{2,0,1:T(8,128)} fusion(bf16[512,8,128]{0,2,1:T(8,128)(2,1)S(1)} %bitcast.38, f32[8,512,512]{2,1,0:T(8,128)S(1)} %fusion.26, pred[512,512]{1,0:T(8,128)(4,1)S(1)} %iota_compare_fusion), kind=kOutput, calls=%fused_computation.28 | convolution fusion | flops 3223322624 | bytes 11796480 | tf_op jit(solution)/shard_map/hts,she->the/dot_general | solution.py:39
  53.3 53.4 %all-to-all-done = bf16[16,1,8,128,128]{4,3,2,1,0:T(8,128)(2,1)} async-done(((bf16[16,1,8,128,128]{4,3,2,1,0:T(8,128)(2,1)}), bf16[16,1,8,128,128]{4,3,2,1,0:T(8,128)(2,1)}, u32[]{:S(2)}, u32[]{:S(2)}) %all-to-all-start) | async-done | bytes 4194336 | tf_op jit(solution)/shard_map/all_to_all | solution.py:12
  106.7 3.4 %fusion = f32[8,128,128]{2,1,0:T(8,128)S(1)} fusion(bf16[16,1,8,128,128]{4,3,2,1,0:T(8,128)(2,1)} %all-to-all-done, pred[16]{0:T(512)(128)(4,1)S(1)} %iota_compare_fusion.1), kind=kLoop, calls=%fused_computation.2 | loop fusion | flops 6160384 | bytes 4718608 | tf_op jit(solution)/shard_map/reduce_sum | solution.py:54
  110.1 0.1 copy-done.7
  110.2 3.3 %multiply_reduce_fusion = (f32[1024,8]{0,1:T(8,128)S(1)}, f32[1024,8,128]{2,0,1:T(8,128)S(1)}) fusion(f32[8,128,128]{2,1,0:T(8,128)S(1)} %fusion, bf16[1024,8,128]{0,2,1:T(8,128)(2,1)S(1)} %bitcast.36, f32[512,8,128]{2,0,1:T(8,128)S(1)} %copy-done.6, f32[512,8,128]{2,0,1:T(8,128)S(1)} %copy-done.7), kind=kOutput, calls=%fused_computation.21 | convolution fusion | flops 1614798848 | bytes 11042816 | tf_op jit(solution)/shard_map/thd,hde->the/dot_general | solution.py:55
  113.5 1.4 multiply_convert_fusion
  114.9 2.7 %copy.80 = bf16[1024,8,128]{0,2,1:T(8,128)(2,1)} copy(bf16[1024,8,128]{2,0,1:T(8,128)(2,1)S(1)} %multiply_convert_fusion) | data formatting | bytes 4194304 | tf_op jit(solution)/shard_map/convert_element_type | solution.py:60
  117.6 40.3 %all-gather.2.cloned.1.call-done = bf16[1024,6144]{1,0:T(8,128)(2,1)} async-done(((bf16[1024,384]{1,0:T(8,128)(2,1)}), bf16[1024,6144]{1,0:T(8,128)(2,1)}) %all-gather.2.cloned.1.call-update) | async-done | bytes 12582928 | tf_op jit(solution)/shard_map/all_gather | solution.py:61
  157.9 21.0 %convolution_convert_fusion = bf16[1024,6144]{1,0:T(8,128)(2,1)} fusion(bf16[1024,1024]{0,1:T(8,128)(2,1)} %bitcast.48, bf16[1024,6144]{1,0:T(8,128)(2,1)} %all-gather.2.cloned.1.call-done), kind=kOutput, calls=%fused_computation | convolution fusion | flops 12891193344 | bytes 27262976 | tf_op jit(solution)/shard_map/dot_general | solution.py:63
  178.9 0.0 reduce-scatter.2.cloned.1.call-update
  179.0 69.9 %reduce-scatter.2.cloned.1.call-done = bf16[128,6144]{1,0:T(8,128)(2,1)} async-done(((bf16[1024,6144]{1,0:T(8,128)(2,1)}), bf16[128,6144]{1,0:T(8,128)(2,1)}) %reduce-scatter.2.cloned.1.call-update) | async-done | bytes 1572880 | tf_op jit(solution)/shard_map/reduce_scatter | solution.py:62
  248.9 2.9 %add_convert_fusion = bf16[128,6144]{1,0:T(8,128)(2,1)} fusion(bf16[128,6144]{1,0:T(8,128)(2,1)S(1)} %copy-done.10, bf16[128,6144]{1,0:T(8,128)(2,1)} %reduce-scatter.2.cloned.1.call-done), kind=kLoop, calls=%fused_computation.26 | loop fusion | flops 3145728 | bytes 4718592 | tf_op jit(solution)/shard_map/convert_element_type | solution.py:68
  (10 shorter events, 0.0 us)
Async XLA Ops:
  6.5 151.4 %all-gather.2.cloned.1.call-start = ((), (), s32[]{:S(2)}) async-start(), calls=%async_computation.2 | async-start | bytes 13369344 | tf_op jit(solution)/shard_map/all_gather | solution.py:61
  13.5 4.0 %copy-start = (bf16[512,1024]{0,1:T(8,128)(2,1)}, bf16[512,1024]{0,1:T(8,128)(2,1)S(1)}, u32[]{:S(2)}) copy-start(bf16[512,1024]{0,1:T(8,128)(2,1)S(1)} %copy.96) | copy-start | bytes 3145732
  17.0 1.0 copy-start.4
  17.0 5.0 %copy-start.2 = (bf16[512,1024]{0,1:T(8,128)(2,1)}, bf16[512,1024]{0,1:T(8,128)(2,1)S(1)}, u32[]{:S(2)}) copy-start(bf16[512,1024]{0,1:T(8,128)(2,1)S(1)} %get-tuple-element.9) | copy-start | bytes 3145732
  17.5 1.1 copy-start.8
  22.0 84.7 %all-to-all-start = ((bf16[16,1,8,128,128]{4,3,2,1,0:T(8,128)(2,1)}), bf16[16,1,8,128,128]{4,3,2,1,0:T(8,128)(2,1)}, u32[]{:S(2)}, u32[]{:S(2)}) async-start(bf16[16,1,8,128,128]{4,3,2,1,0:T(8,128)(2,1)} %stack.2), calls=%async_computation | async-start | bytes 8388608 | tf_op jit(solution)/shard_map/all_to_all | solution.py:12
  30.5 218.4 %reduce-scatter.2.cloned.1.call-start = ((), (), s32[]{:S(2)}) async-start(), calls=%async_computation.3 | async-start | bytes 14155776 | tf_op jit(solution)/shard_map/reduce_scatter | solution.py:62
  34.6 3.1 %copy-start.5 = (bf16[512,1024]{0,1:T(8,128)(2,1)S(1)}, bf16[512,1024]{0,1:T(8,128)(2,1)}, u32[]{:S(2)}) copy-start(bf16[512,1024]{0,1:T(8,128)(2,1)} %copy-done.4) | copy-start | bytes 3145732
  37.7 1.3 copy-start.1
  39.0 4.6 %copy-start.9 = (f32[8,128,128]{2,1,0:T(8,128)S(1)}, f32[8,128,128]{2,1,0:T(8,128)}, u32[]{:S(2)}) copy-start(f32[8,128,128]{2,1,0:T(8,128)} %copy-done.8) | copy-start | bytes 1572868
  43.6 2.5 copy-start.3
  106.7 3.4 %copy-start.6 = (f32[512,8,128]{2,0,1:T(8,128)S(1)}, f32[512,8,128]{2,0,1:T(8,128)}, u32[]{:S(2)}) copy-start(f32[512,8,128]{2,0,1:T(8,128)} %bitcast_add_fusion) | copy-start | bytes 6291460
  106.7 3.5 %copy-start.7 = (f32[512,8,128]{2,0,1:T(8,128)S(1)}, f32[512,8,128]{2,0,1:T(8,128)}, u32[]{:S(2)}) copy-start(f32[512,8,128]{2,0,1:T(8,128)} %fusion.17) | copy-start | bytes 6291460
  110.2 3.3 %copy-start.11 = (f32[1024]{0:T(1024)S(1)}, f32[1024]{0:T(1024)}, u32[]{:S(2)}) copy-start(f32[1024]{0:T(1024)} %param.9) | copy-start | bytes 12292
  178.9 69.9 %copy-start.10 = (bf16[128,6144]{1,0:T(8,128)(2,1)S(1)}, bf16[128,6144]{1,0:T(8,128)(2,1)}, u32[]{:S(2)}) copy-start(bf16[128,6144]{1,0:T(8,128)(2,1)} %param.11) | copy-start | bytes 4718596
Sparse Core Ops, SparseCore 0:
  9.5 148.3 all-gather.1
  179.1 69.7 reduce-scatter.1
